TPU v7x, 32 devices: a whole 2x2x4 slice. The times are simulated.
32 devices in a mesh: base: 16 (over z, x, core), band: 2 (over y).
Axes of the slice: x: 2, y: 2, z: 4, core: 2. Of those that a mesh axis runs over, the one named last changes fastest.
Arguments:
- coherency: float32 [16, 16, 8, 4096], P('band', None, None, 'base'), may hold values from -1.5 to 1.5
- observed: float32 [16, 8, 4096], P('band', None, 'base'), may hold values from -6 to 6
- jones_deviation: float32 [16, 16, 8, 512], P('band', None, None, 'base'), may hold values from -1.8 to 1.8
- antenna_first: int32 [4096], P('base'), may hold values from 0 to 511, as said below
- antenna_second: int32 [4096], P('base'), may hold values from 0 to 511, as said below
Outputs:
- jones: float32 [16, 16, 8, 512], P('band', None, None, 'base')
- residual: float32 [16, 8, 4096], P('band', None, 'base')
Inputs may be any that keep to these rules, and one draw needn't show every extreme that they name: `antenna_first`: every station is the first station of exactly 8 baselines. On every baseline antenna_second differs from antenna_first.
All inputs are finite; a program needn't handle non-finite values.
Results may differ from a plain program's by a relative error of at most 0.0003.
Values sent between devices are 32-bit elements; how exact they have to be, the bound alone decides.
A program may use at most 128 MiB of HBM per device.

v0:
```python
import jax
import jax.numpy as jnp
from jax import lax
from jax.sharding import PartitionSpec as P

ITERS = 3
step_gain = 1.2
penalty_gain = 0.25


def expand_matrix(packed):
    return [
        [(packed[..., 0, :], packed[..., 1, :]), (packed[..., 2, :], packed[..., 3, :])],
        [(packed[..., 4, :], packed[..., 5, :]), (packed[..., 6, :], packed[..., 7, :])],
    ]


def pack_matrix(matrix):
    return jnp.stack(
        [
            matrix[0][0][0],
            matrix[0][0][1],
            matrix[0][1][0],
            matrix[0][1][1],
            matrix[1][0][0],
            matrix[1][0][1],
            matrix[1][1][0],
            matrix[1][1][1],
        ],
        axis=-2,
    )


def complex_mul(first_term, second_term):
    return (
        first_term[0] * second_term[0] - first_term[1] * second_term[1],
        first_term[0] * second_term[1] + first_term[1] * second_term[0],
    )


def complex_add(first_term, second_term):
    return (first_term[0] + second_term[0], first_term[1] + second_term[1])


def element_of(matrix, i, j, adjoint):
    if adjoint:
        return (matrix[j][i][0], -matrix[j][i][1])
    return matrix[i][j]


def matrix_product(first_factor, second_factor, adjoint_first=False, adjoint_second=False):
    result_rows = []
    for i in range(2):
        row_items = []
        for j in range(2):
            row_items.append(
                complex_add(
                    complex_mul(
                        element_of(first_factor, i, 0, adjoint_first),
                        element_of(second_factor, 0, j, adjoint_second),
                    ),
                    complex_mul(
                        element_of(first_factor, i, 1, adjoint_first),
                        element_of(second_factor, 1, j, adjoint_second),
                    ),
                )
            )
        result_rows.append(row_items)
    return result_rows


def fit_basis(band_count):
    positions = (2.0 * jnp.arange(band_count, dtype=jnp.float32) + 1.0) / band_count - 1.0
    columns = []
    for power in range(4):
        vector = positions**power
        for earlier in columns:
            vector = vector - jnp.sum(earlier * vector) * earlier
        vector = vector / jnp.sqrt(jnp.sum(vector * vector))
        columns.append(vector)
    return jnp.stack(columns, axis=1)


def local_gradients(
    leading_rows, trailing_rows, coherency, observed, antenna_first, antenna_second, station_number
):
    leading_jones = expand_matrix(leading_rows)
    trailing_jones = expand_matrix(trailing_rows)
    sky = expand_matrix(coherency)
    model = pack_matrix(
        matrix_product(leading_jones, matrix_product(sky, trailing_jones, adjoint_second=True))
    )
    residual = observed - jnp.sum(model, axis=1)
    resid_parts = expand_matrix(residual[:, None])
    gradient_leading = pack_matrix(
        matrix_product(resid_parts, matrix_product(trailing_jones, sky, adjoint_second=True))
    )
    gradient_trailing = pack_matrix(
        matrix_product(resid_parts, matrix_product(leading_jones, sky), adjoint_first=True)
    )
    shape_out = (coherency.shape[0], coherency.shape[1], 8, station_number)
    gradient_list = (
        jnp.zeros(shape_out, jnp.float32)
        .at[:, :, :, antenna_first]
        .add(gradient_leading)
        .at[:, :, :, antenna_second]
        .add(gradient_trailing)
    )
    return (gradient_list, residual)


def per_device(coherency, observed, jones_deviation, antenna_first, antenna_second):
    highest = lax.Precision.HIGHEST
    base_count = lax.axis_size("base")
    band_count = lax.axis_size("band")
    sub_dev = coherency.shape[0]
    base_dev = coherency.shape[-1]
    own_stations = jones_deviation.shape[-1]
    station_number = own_stations * base_count
    baseline_count = base_dev * base_count
    step_size = step_gain * station_number / baseline_count
    penalty = penalty_gain * baseline_count / station_number
    poly_basis = fit_basis(sub_dev * band_count)
    local_basis = lax.dynamic_slice_in_dim(poly_basis, lax.axis_index("band") * sub_dev, sub_dev, 0)
    identity = jnp.array([1.0, 0.0, 0.0, 0.0, 0.0, 0.0, 1.0, 0.0], dtype=jnp.float32)[:, None]
    jones_current = identity + jones_deviation
    jones_current = lax.all_gather(jones_current, "base", axis=3, tiled=True)
    consensus = jones_current
    dual_var = jnp.zeros_like(jones_current)
    residual = None
    for iteration in range(ITERS):
        leading_rows = jnp.take(jones_current, antenna_first, axis=3)
        trailing_rows = jnp.take(jones_current, antenna_second, axis=3)
        local_terms, residual = local_gradients(
            leading_rows,
            trailing_rows,
            coherency,
            observed,
            antenna_first,
            antenna_second,
            station_number,
        )
        station_gradients = lax.psum(local_terms, "base")
        jones_current = jones_current + step_size * (
            station_gradients - dual_var - penalty * (jones_current - consensus)
        )
        if iteration + 1 < ITERS:
            target = jones_current + dual_var / penalty
            partial_fit = jnp.einsum("fm,fkcs->mkcs", local_basis, target, precision=highest)
            coefficients = lax.psum(partial_fit, "band")
            consensus = jnp.einsum("fm,mkcs->fkcs", local_basis, coefficients, precision=highest)
            dual_var = dual_var + penalty * (jones_current - consensus)
    jones_current = lax.dynamic_slice_in_dim(
        jones_current, lax.axis_index("base") * own_stations, own_stations, 3
    )
    return (jones_current, residual)


def solution(mesh):
    return jax.shard_map(
        per_device,
        mesh=mesh,
        in_specs=(
            P("band", None, None, "base"),
            P("band", None, "base"),
            P("band", None, None, "base"),
            P("base"),
            P("base"),
        ),
        out_specs=(P("band", None, None, "base"), P("band", None, "base")),
        check_vma=False,
    )
```

profile of v0, /device:TPU:0, one launch (start us, length us, event | category | flops | bytes accessed | tf_op | source)
XLA Modules:
  0.0 1139.3 jit_solution(16276159739745969013)
XLA Ops:
  19.4 120.1 %all-gather.2.cloned.1.call-done = f32[8,16,8,512]{1,2,0,3:T(8,128)} async-done(((f32[8,16,8,32]{1,2,0,3:T(8,128)}), f32[8,16,8,512]{1,2,0,3:T(8,128)}) %all-gather.2.cloned.1.call-update) | async-done | bytes 2097168 | tf_op jit(solution)/shard_map/all_gather | solution.py:127
  139.5 11.4 copy.497
  150.9 10.6 gather_fusion
  168.6 10.6 gather_fusion.1
  254.8 39.8 %scatter_fusion = f32[8,16,8,512]{1,2,3,0:T(8,128)} fusion(f32[8,16,8,512]{1,2,3,0:T(8,128)} %broadcast.414.clone, s32[256]{0:T(256)S(1)} %copy-done.42, f32[256,8,16,8]{2,3,1,0:T(8,128)} %copy.527), kind=kCustom, calls=%fused_computation.6 | custom fusion | flops 262144 | bytes 3146752 | tf_op jit(solution)/shard_map/scatter-add | solution.py:105
  294.7 39.9 %scatter_fusion.1 = f32[8,16,8,512]{1,2,3,0:T(8,128)} fusion(f32[8,16,8,512]{1,2,3,0:T(8,128)} %scatter_fusion, s32[256]{0:T(256)S(1)} %copy-done.38, f32[256,8,16,8]{2,3,1,0:T(8,128)} %copy.536), kind=kCustom, calls=%fused_computation.7 | custom fusion | flops 262144 | bytes 3146752 | tf_op jit(solution)/shard_map/scatter-add | solution.py:107
  334.6 9.7 copy.537
  350.6 12.2 %copy.540 = f32[8,16,8,512]{3,0,2,1:T(8,128)} copy(f32[8,16,8,512]{1,2,0,3:T(8,128)} %all-gather.2.cloned.1.call-done) | data formatting | bytes 4194304 | tf_op jit(solution)/shard_map/all_gather | solution.py:127
  362.8 78.2 %all-reduce.6.cloned.1.call-done = f32[8,16,8,512]{3,0,2,1:T(8,128)} async-done(((f32[8,16,8,512]{3,0,2,1:T(8,128)}), f32[8,16,8,512]{3,0,2,1:T(8,128)}) %all-reduce.6.cloned.1.call-update) | async-done | bytes 2097168 | tf_op jit(solution)/shard_map/psum | solution.py:143
  443.8 7.8 copy.541
  451.6 10.8 gather_fusion.2
  462.4 10.8 gather_fusion.3
  586.2 39.8 %scatter_fusion.2 = f32[8,16,8,512]{1,2,3,0:T(8,128)} fusion(f32[8,16,8,512]{1,2,3,0:T(8,128)} %broadcast.414.clone.1, s32[256]{0:T(256)S(1)} %copy-done.43, f32[256,8,16,8]{2,3,1,0:T(8,128)} %copy.563), kind=kCustom, calls=%fused_computation.8 | custom fusion | flops 262144 | bytes 3146752 | tf_op jit(solution)/shard_map/scatter-add | solution.py:105
  626.0 39.8 %scatter_fusion.3 = f32[8,16,8,512]{1,2,3,0:T(8,128)} fusion(f32[8,16,8,512]{1,2,3,0:T(8,128)} %scatter_fusion.2, s32[256]{0:T(256)S(1)} %copy-done.39, f32[256,8,16,8]{2,3,1,0:T(8,128)} %copy.572), kind=kCustom, calls=%fused_computation.9 | custom fusion | flops 262144 | bytes 3146752 | tf_op jit(solution)/shard_map/scatter-add | solution.py:107
  665.8 9.7 copy.573
  686.7 86.7 %all-reduce.8.cloned.1.call-done = f32[8,16,8,512]{3,0,2,1:T(8,128)} async-done(((f32[8,16,8,512]{3,0,2,1:T(8,128)}), f32[8,16,8,512]{3,0,2,1:T(8,128)}) %all-reduce.8.cloned.1.call-update) | async-done | bytes 2097168 | tf_op jit(solution)/shard_map/psum | solution.py:143
  773.5 41.6 %all-reduce.10.cloned.1.call-done = f32[4,16,8,512]{3,0,2,1:T(4,128)} async-done(((f32[4,16,8,512]{3,0,2,1:T(4,128)}), f32[4,16,8,512]{3,0,2,1:T(4,128)}) %all-reduce.10.cloned.1.call-update) | async-done | bytes 1048592 | tf_op jit(solution)/shard_map/psum | solution.py:150
  828.8 10.8 gather_fusion.4
  839.6 10.8 gather_fusion.5
  912.8 8.4 copy.596
  940.7 39.8 %scatter_fusion.4 = f32[8,16,8,512]{1,2,3,0:T(8,128)} fusion(f32[8,16,8,512]{1,2,3,0:T(8,128)} %broadcast.414, s32[256]{0:T(256)S(1)} %copy-done.44, f32[256,8,16,8]{2,3,1,0:T(8,128)} %copy.596), kind=kCustom, calls=%fused_computation.10 | custom fusion | flops 262144 | bytes 3146752 | tf_op jit(solution)/shard_map/scatter-add | solution.py:105
  980.5 39.8 %scatter_fusion.5 = f32[8,16,8,512]{1,2,3,0:T(8,128)} fusion(f32[8,16,8,512]{1,2,3,0:T(8,128)} %scatter_fusion.4, s32[256]{0:T(256)S(1)} %copy-done.40, f32[256,8,16,8]{2,3,1,0:T(8,128)} %copy.605), kind=kCustom, calls=%fused_computation.11 | custom fusion | flops 262144 | bytes 3146752 | tf_op jit(solution)/shard_map/scatter-add | solution.py:107
  1020.3 10.1 copy.606
  1036.3 92.8 %all-reduce.12.cloned.1.call-done = f32[8,16,8,512]{3,0,2,1:T(8,128)} async-done(((f32[8,16,8,512]{3,0,2,1:T(8,128)}), f32[8,16,8,512]{3,0,2,1:T(8,128)}) %all-reduce.12.cloned.1.call-update) | async-done | bytes 2097168 | tf_op jit(solution)/shard_map/psum | solution.py:143
  (313 shorter events, 327.9 us)
Async XLA Ops:
  7.2 132.3 %all-gather.2.cloned.1.call-start = ((), (), s32[]{:S(2)}) async-start(), calls=%async_computation | async-start | bytes 17825792 | tf_op jit(solution)/shard_map/all_gather | solution.py:127
  10.2 430.8 %all-reduce.6.cloned.1.call-start = ((), (), s32[]{:S(2)}) async-start(), calls=%async_computation.1 | async-start | bytes 4194304 | tf_op jit(solution)/shard_map/psum | solution.py:143
  11.5 187.3 %copy-start.13 = (f32[8,8,256]{1,0,2:T(8,128)}, f32[8,8,256]{1,0,2:T(8,128)S(1)}, u32[]{:S(2)}) copy-start(f32[8,8,256]{1,0,2:T(8,128)S(1)} %copy.510) | copy-start | bytes 196612
  12.3 138.6 %copy-start.45 = (s32[1024]{0:T(1024)}, s32[1024]{0:T(1024)S(1)}, u32[]{:S(2)}) copy-start(s32[1024]{0:T(1024)S(1)} %pad_clamp_fusion.1) | copy-start | bytes 12292
  12.9 155.8 %copy-start.46 = (s32[1024]{0:T(1024)}, s32[1024]{0:T(1024)S(1)}, u32[]{:S(2)}) copy-start(s32[1024]{0:T(1024)S(1)} %pad_clamp_fusion) | copy-start | bytes 12292
  13.6 173.3 %copy-start.50 = (pred[256]{0:T(512)(128)(4,1)}, pred[256]{0:T(512)(128)(4,1)S(1)}, u32[]{:S(2)}) copy-start(pred[256]{0:T(512)(128)(4,1)S(1)} %get-tuple-element.206) | copy-start | bytes 772
  13.6 174.7 %copy-start.47 = (pred[256]{0:T(512)(128)(4,1)}, pred[256]{0:T(512)(128)(4,1)S(1)}, u32[]{:S(2)}) copy-start(pred[256]{0:T(512)(128)(4,1)S(1)} %get-tuple-element.205) | copy-start | bytes 772
  19.3 198.3 %copy-start.5 = (f32[8,16,1,256]{3,2,1,0:T(1,128)}, f32[8,16,1,256]{3,2,1,0:T(1,128)S(1)}, u32[]{:S(2)}) copy-start(f32[8,16,1,256]{3,2,1,0:T(1,128)S(1)} %get-tuple-element.140) | copy-start | bytes 393220
  19.3 198.3 %copy-start.7 = (f32[8,16,1,256]{3,2,1,0:T(1,128)}, f32[8,16,1,256]{3,2,1,0:T(1,128)S(1)}, u32[]{:S(2)}) copy-start(f32[8,16,1,256]{3,2,1,0:T(1,128)S(1)} %get-tuple-element.142) | copy-start | bytes 393220
  19.4 198.3 %copy-start.9 = (f32[8,16,1,256]{3,2,1,0:T(1,128)}, f32[8,16,1,256]{3,2,1,0:T(1,128)S(1)}, u32[]{:S(2)}) copy-start(f32[8,16,1,256]{3,2,1,0:T(1,128)S(1)} %get-tuple-element.145) | copy-start | bytes 393220
  19.4 198.3 %copy-start.11 = (f32[8,16,1,256]{3,2,1,0:T(1,128)}, f32[8,16,1,256]{3,2,1,0:T(1,128)S(1)}, u32[]{:S(2)}) copy-start(f32[8,16,1,256]{3,2,1,0:T(1,128)S(1)} %get-tuple-element.146) | copy-start | bytes 393220
  19.4 199.8 %copy-start.3 = (f32[8,16,1,256]{3,2,1,0:T(1,128)}, f32[8,16,1,256]{3,2,1,0:T(1,128)S(1)}, u32[]{:S(2)}) copy-start(f32[8,16,1,256]{3,2,1,0:T(1,128)S(1)} %get-tuple-element.147) | copy-start | bytes 393220
  247.8 46.9 %copy-start.38 = (s32[256]{0:T(256)S(1)}, s32[256]{0:T(256)}, u32[]{:S(2)}) copy-start(s32[256]{0:T(256)} %copy-done.37) | copy-start | bytes 3076
  344.3 429.2 %all-reduce.8.cloned.1.call-start = ((), (), s32[]{:S(2)}) async-start(), calls=%async_computation.2 | async-start | bytes 4194304 | tf_op jit(solution)/shard_map/psum | solution.py:143
  443.8 240.0 %copy-start.2 = (f32[8,16,8,512]{3,0,2,1:T(8,128)}, f32[8,16,8,512]{3,0,2,1:T(8,128)S(1)}, u32[]{:S(2)}) copy-start(f32[8,16,8,512]{3,0,2,1:T(8,128)S(1)} %multiply_add_fusion) | copy-start | bytes 6291460
  451.6 28.7 %copy-start.51 = (pred[256]{0:T(512)(128)(4,1)S(1)}, pred[256]{0:T(512)(128)(4,1)}, u32[]{:S(2)}) copy-start(pred[256]{0:T(512)(128)(4,1)} %copy-done.50) | copy-start | bytes 772
  473.2 16.0 %copy-start.48 = (pred[256]{0:T(512)(128)(4,1)S(1)}, pred[256]{0:T(512)(128)(4,1)}, u32[]{:S(2)}) copy-start(pred[256]{0:T(512)(128)(4,1)} %copy-done.47) | copy-start | bytes 772
  579.1 46.9 %copy-start.39 = (s32[256]{0:T(256)S(1)}, s32[256]{0:T(256)}, u32[]{:S(2)}) copy-start(s32[256]{0:T(256)} %copy-done.37) | copy-start | bytes 3076
  675.5 139.5 %all-reduce.10.cloned.1.call-start = ((), (), s32[]{:S(2)}) async-start(), calls=%async_computation.3 | async-start | bytes 2097152 | tf_op jit(solution)/shard_map/psum | solution.py:150
  683.8 145.0 %copy-start.35 = (f32[16,4]{0,1:T(4,128)}, f32[16,4]{0,1:T(4,128)S(1)}, u32[]{:S(2)}) copy-start(f32[16,4]{0,1:T(4,128)S(1)} %pad_maximum_fusion) | copy-start | bytes 772
  686.7 344.7 %all-reduce.14.cloned.1.call-start = ((), (), s32[]{:S(2)}) async-start(), calls=%async_computation.5 | async-start | bytes 2097152 | tf_op jit(solution)/shard_map/psum | solution.py:150
  828.8 27.8 %copy-start.52 = (pred[256]{0:T(512)(128)(4,1)S(1)}, pred[256]{0:T(512)(128)(4,1)}, u32[]{:S(2)}) copy-start(pred[256]{0:T(512)(128)(4,1)} %copy-done.50) | copy-start | bytes 772
  900.9 228.2 %all-reduce.12.cloned.1.call-start = ((), (), s32[]{:S(2)}) async-start(), calls=%async_computation.4 | async-start | bytes 4194304 | tf_op jit(solution)/shard_map/psum | solution.py:143
  933.6 46.9 %copy-start.40 = (s32[256]{0:T(256)S(1)}, s32[256]{0:T(256)}, u32[]{:S(2)}) copy-start(s32[256]{0:T(256)} %copy-done.37) | copy-start | bytes 3076
  (36 other events, 244.2 us)
Sparse Core Ops, SparseCore 0:
  10.3 129.1 all-gather.1
  344.4 96.5 all-reduce.5
  675.6 97.8 all-reduce.7
  775.6 39.3 all-reduce.9
  901.0 40.0 all-reduce.13
  1030.6 98.4 all-reduce.11
where the time goes:
time: 1150 us; the launch traced here: 1140 us
  waiting for transfers between devices  419 us (36%)
  local copies, waits for them, and re-layouts  357 us (31%)
  other arithmetic  324 us (28%)
  between operations  19.6 us (2%)
  matrix products  18.7 us (2%)
    psum x3, waiting for transfers between devices, per_device(): station_gradients = lax.psum(local_terms, 'base')  258 us
    scatter-add x6, other arithmetic, local_gradients(): gradient_list = jnp.zeros(shape_out, jnp.float32).at[:, :, :, antenna_fir...  239 us
    all_gather x1, waiting for transfers between devices, per_device(): jones_current = lax.all_gather(jones_current, 'base', axis=3, tiled=True)  120 us
    another operation x12, local copies, waits for them, and re-layouts, pack_matrix(): jnp.stack([matrix[0][0][0], matrix[0][0][1], matrix[0][1][0], matrix[0][1...  61.1 us
    gather x6, local copies, waits for them, and re-layouts, per_device(): trailing_rows = jnp.take(jones_current, antenna_second, axis=3)  53.9 us
    gather x6, local copies, waits for them, and re-layouts, per_device(): leading_rows = jnp.take(jones_current, antenna_first, axis=3)  52.7 us
    psum x2, waiting for transfers between devices, per_device(): coefficients = lax.psum(partial_fit, 'band')  41.6 us
    scatter-add x3, local copies, waits for them, and re-layouts, local_gradients(): gradient_list = jnp.zeros(shape_out, jnp.float32).at[:, :, :, antenna_fir...  29.5 us
  transfers between devices with their start and end apart: 6, of which 5 were waited for; matrix products, arithmetic and copies ran while one was open for 15% of the time, Pallas kernels for 0%

commit v1 on v0

--- a/solution.py
+++ b/solution.py
@@ -2,6 +2,7 @@
 import jax.numpy as jnp
 from jax import lax
 from jax.sharding import PartitionSpec as P
+from jax.lax import all_gather
 
 ITERS = 3
 step_gain = 1.2
@@ -124,7 +125,7 @@
     local_basis = lax.dynamic_slice_in_dim(poly_basis, lax.axis_index("band") * sub_dev, sub_dev, 0)
     identity = jnp.array([1.0, 0.0, 0.0, 0.0, 0.0, 0.0, 1.0, 0.0], dtype=jnp.float32)[:, None]
     jones_current = identity + jones_deviation
-    jones_current = lax.all_gather(jones_current, "base", axis=3, tiled=True)
+    jones_current = jnp.concatenate(all_gather(jones_current, "base"), axis=3)
     consensus = jones_current
     dual_var = jnp.zeros_like(jones_current)
     residual = None

time: 1150 us -> 1120 us (0.974)
  waiting for transfers between devices: 419 us -> 380 us
    all_gather x1, waiting for transfers between devices: 120 us -> 68.3 us  [per_device(): jones_current = jnp.concatenate(all_gather(jones_current, 'base'), axis=3)]
    reshape x0 -> x2, local copies, waits for them, and re-layouts: none -> 16.3 us  [per_device(): jones_current = jnp.concatenate(all_gather(jones_current, 'base'), axis=3)]
    psum x3, waiting for transfers between devices: 258 us -> 270 us  [per_device(): station_gradients = lax.psum(local_terms, 'base')]
    all_gather x2 -> x1, local copies, waits for them, and re-layouts: 23.6 us -> 11.5 us  [per_device(): jones_current = jnp.concatenate(all_gather(jones_current, 'base'), axis=3)]
  transfers between devices with their start and end apart: 6 -> 6, of which waited for: 5 -> 5; matrix products, arithmetic and copies ran while one was open for 15% -> 14% of each run, Pallas kernels for 0% -> 0%
where the time goes in v1:
time: 1120 us; the launch traced here: 1100 us
  waiting for transfers between devices  380 us (34%)
  local copies, waits for them, and re-layouts  360 us (32%)
  other arithmetic  325 us (29%)
  between operations  19.5 us (2%)
  matrix products  18.7 us (2%)
    psum x3, waiting for transfers between devices, per_device(): station_gradients = lax.psum(local_terms, 'base')  270 us
    scatter-add x6, other arithmetic, local_gradients(): gradient_list = jnp.zeros(shape_out, jnp.float32).at[:, :, :, antenna_fir...  239 us
    all_gather x1, waiting for transfers between devices, per_device(): jones_current = jnp.concatenate(all_gather(jones_current, 'base'), axis=3)  68.3 us
    another operation x12, local copies, waits for them, and re-layouts, pack_matrix(): jnp.stack([matrix[0][0][0], matrix[0][0][1], matrix[0][1][0], matrix[0][1...  61.1 us
    gather x6, local copies, waits for them, and re-layouts, per_device(): trailing_rows = jnp.take(jones_current, antenna_second, axis=3)  53.8 us
    gather x6, local copies, waits for them, and re-layouts, per_device(): leading_rows = jnp.take(jones_current, antenna_first, axis=3)  52.7 us
    psum x2, waiting for transfers between devices, per_device(): coefficients = lax.psum(partial_fit, 'band')  41.6 us
    scatter-add x3, local copies, waits for them, and re-layouts, local_gradients(): gradient_list = jnp.zeros(shape_out, jnp.float32).at[:, :, :, antenna_fir...  29.5 us
  transfers between devices with their start and end apart: 6, of which 5 were waited for; matrix products, arithmetic and copies ran while one was open for 14% of the time, Pallas kernels for 0%

profile of v1, /device:TPU:0, one launch (start us, length us, event | category | flops | bytes accessed | tf_op | source)
XLA Modules:
  0.0 1104.2 jit_solution(9750144865507982161)
XLA Ops:
  19.4 68.3 %all-gather.3.cloned.1.call-done = f32[128,16,8,32]{3,2,1,0:T(8,128)} async-done(((f32[8,16,8,32]{3,2,1,0:T(8,128)}), f32[128,16,8,32]{3,2,1,0:T(8,128)}) %all-gather.3.cloned.1.call-update) | async-done | bytes 2097168 | tf_op jit(solution)/shard_map/all_gather | solution.py:128
  87.8 11.5 %copy.1186 = f32[16,8,16,8,32]{4,0,1,3,2:T(8,128)} copy(f32[16,8,16,8,32]{4,3,2,1,0:T(8,128)} %bitcast.86) | data formatting | bytes 4194304 | tf_op jit(solution)/shard_map/all_gather | solution.py:128
  106.8 8.7 copy.488
  115.5 10.7 gather_fusion
  133.3 10.7 gather_fusion.1
  219.4 39.8 %scatter_fusion = f32[8,16,8,512]{1,2,3,0:T(8,128)} fusion(f32[8,16,8,512]{1,2,3,0:T(8,128)} %broadcast.414.clone, s32[256]{0:T(256)S(1)} %copy-done.42, f32[256,8,16,8]{2,3,1,0:T(8,128)} %copy.518), kind=kCustom, calls=%fused_computation.6 | custom fusion | flops 262144 | bytes 3146752 | tf_op jit(solution)/shard_map/scatter-add | solution.py:106
  259.2 39.8 %scatter_fusion.1 = f32[8,16,8,512]{1,2,3,0:T(8,128)} fusion(f32[8,16,8,512]{1,2,3,0:T(8,128)} %scatter_fusion, s32[256]{0:T(256)S(1)} %copy-done.38, f32[256,8,16,8]{2,3,1,0:T(8,128)} %copy.527), kind=kCustom, calls=%fused_computation.7 | custom fusion | flops 262144 | bytes 3146752 | tf_op jit(solution)/shard_map/scatter-add | solution.py:108
  299.0 9.7 copy.528
  315.1 90.8 %all-reduce.6.cloned.1.call-done = f32[8,16,8,512]{3,0,2,1:T(8,128)} async-done(((f32[8,16,8,512]{3,0,2,1:T(8,128)}), f32[8,16,8,512]{3,0,2,1:T(8,128)}) %all-reduce.6.cloned.1.call-update) | async-done | bytes 2097168 | tf_op jit(solution)/shard_map/psum | solution.py:144
  408.8 7.8 copy.529
  416.5 10.8 gather_fusion.2
  427.3 10.8 gather_fusion.3
  551.1 39.8 %scatter_fusion.2 = f32[8,16,8,512]{1,2,3,0:T(8,128)} fusion(f32[8,16,8,512]{1,2,3,0:T(8,128)} %broadcast.414.clone.1, s32[256]{0:T(256)S(1)} %copy-done.43, f32[256,8,16,8]{2,3,1,0:T(8,128)} %copy.551), kind=kCustom, calls=%fused_computation.8 | custom fusion | flops 262144 | bytes 3146752 | tf_op jit(solution)/shard_map/scatter-add | solution.py:106
  590.8 39.8 %scatter_fusion.3 = f32[8,16,8,512]{1,2,3,0:T(8,128)} fusion(f32[8,16,8,512]{1,2,3,0:T(8,128)} %scatter_fusion.2, s32[256]{0:T(256)S(1)} %copy-done.39, f32[256,8,16,8]{2,3,1,0:T(8,128)} %copy.560), kind=kCustom, calls=%fused_computation.9 | custom fusion | flops 262144 | bytes 3146752 | tf_op jit(solution)/shard_map/scatter-add | solution.py:108
  630.6 9.7 copy.561
  651.8 86.5 %all-reduce.8.cloned.1.call-done = f32[8,16,8,512]{3,0,2,1:T(8,128)} async-done(((f32[8,16,8,512]{3,0,2,1:T(8,128)}), f32[8,16,8,512]{3,0,2,1:T(8,128)}) %all-reduce.8.cloned.1.call-update) | async-done | bytes 2097168 | tf_op jit(solution)/shard_map/psum | solution.py:144
  738.3 41.6 %all-reduce.10.cloned.1.call-done = f32[4,16,8,512]{3,0,2,1:T(4,128)} async-done(((f32[4,16,8,512]{3,0,2,1:T(4,128)}), f32[4,16,8,512]{3,0,2,1:T(4,128)}) %all-reduce.10.cloned.1.call-update) | async-done | bytes 1048592 | tf_op jit(solution)/shard_map/psum | solution.py:151
  793.6 10.8 gather_fusion.4
  804.5 10.8 gather_fusion.5
  877.7 8.4 copy.584
  905.6 39.8 %scatter_fusion.4 = f32[8,16,8,512]{1,2,3,0:T(8,128)} fusion(f32[8,16,8,512]{1,2,3,0:T(8,128)} %broadcast.414, s32[256]{0:T(256)S(1)} %copy-done.44, f32[256,8,16,8]{2,3,1,0:T(8,128)} %copy.584), kind=kCustom, calls=%fused_computation.10 | custom fusion | flops 262144 | bytes 3146752 | tf_op jit(solution)/shard_map/scatter-add | solution.py:106
  945.4 39.8 %scatter_fusion.5 = f32[8,16,8,512]{1,2,3,0:T(8,128)} fusion(f32[8,16,8,512]{1,2,3,0:T(8,128)} %scatter_fusion.4, s32[256]{0:T(256)S(1)} %copy-done.40, f32[256,8,16,8]{2,3,1,0:T(8,128)} %copy.593), kind=kCustom, calls=%fused_computation.11 | custom fusion | flops 262144 | bytes 3146752 | tf_op jit(solution)/shard_map/scatter-add | solution.py:108
  985.2 10.1 copy.594
  1001.2 92.8 %all-reduce.12.cloned.1.call-done = f32[8,16,8,512]{3,0,2,1:T(8,128)} async-done(((f32[8,16,8,512]{3,0,2,1:T(8,128)}), f32[8,16,8,512]{3,0,2,1:T(8,128)}) %all-reduce.12.cloned.1.call-update) | async-done | bytes 2097168 | tf_op jit(solution)/shard_map/psum | solution.py:144
  (313 shorter events, 335.7 us)
Async XLA Ops:
  7.2 80.6 %all-gather.3.cloned.1.call-start = ((), (), s32[]{:S(2)}) async-start(), calls=%async_computation.5 | async-start | bytes 8912896 | tf_op jit(solution)/shard_map/all_gather | solution.py:128
  9.2 396.7 %all-reduce.6.cloned.1.call-start = ((), (), s32[]{:S(2)}) async-start(), calls=%async_computation | async-start | bytes 4194304 | tf_op jit(solution)/shard_map/psum | solution.py:144
  10.5 152.9 %copy-start.13 = (f32[8,8,256]{1,0,2:T(8,128)}, f32[8,8,256]{1,0,2:T(8,128)S(1)}, u32[]{:S(2)}) copy-start(f32[8,8,256]{1,0,2:T(8,128)S(1)} %copy.501) | copy-start | bytes 196612
  11.3 104.2 %copy-start.45 = (s32[1024]{0:T(1024)}, s32[1024]{0:T(1024)S(1)}, u32[]{:S(2)}) copy-start(s32[1024]{0:T(1024)S(1)} %pad_clamp_fusion.1) | copy-start | bytes 12292
  11.9 121.4 %copy-start.46 = (s32[1024]{0:T(1024)}, s32[1024]{0:T(1024)S(1)}, u32[]{:S(2)}) copy-start(s32[1024]{0:T(1024)S(1)} %pad_clamp_fusion) | copy-start | bytes 12292
  12.6 138.9 %copy-start.50 = (pred[256]{0:T(512)(128)(4,1)}, pred[256]{0:T(512)(128)(4,1)S(1)}, u32[]{:S(2)}) copy-start(pred[256]{0:T(512)(128)(4,1)S(1)} %get-tuple-element.206) | copy-start | bytes 772
  12.6 140.3 %copy-start.47 = (pred[256]{0:T(512)(128)(4,1)}, pred[256]{0:T(512)(128)(4,1)S(1)}, u32[]{:S(2)}) copy-start(pred[256]{0:T(512)(128)(4,1)S(1)} %get-tuple-element.205) | copy-start | bytes 772
  19.4 162.8 %copy-start.5 = (f32[8,16,1,256]{3,2,1,0:T(1,128)}, f32[8,16,1,256]{3,2,1,0:T(1,128)S(1)}, u32[]{:S(2)}) copy-start(f32[8,16,1,256]{3,2,1,0:T(1,128)S(1)} %get-tuple-element.140) | copy-start | bytes 393220
  19.4 162.8 %copy-start.7 = (f32[8,16,1,256]{3,2,1,0:T(1,128)}, f32[8,16,1,256]{3,2,1,0:T(1,128)S(1)}, u32[]{:S(2)}) copy-start(f32[8,16,1,256]{3,2,1,0:T(1,128)S(1)} %get-tuple-element.142) | copy-start | bytes 393220
  19.4 162.8 %copy-start.9 = (f32[8,16,1,256]{3,2,1,0:T(1,128)}, f32[8,16,1,256]{3,2,1,0:T(1,128)S(1)}, u32[]{:S(2)}) copy-start(f32[8,16,1,256]{3,2,1,0:T(1,128)S(1)} %get-tuple-element.145) | copy-start | bytes 393220
  19.4 162.8 %copy-start.11 = (f32[8,16,1,256]{3,2,1,0:T(1,128)}, f32[8,16,1,256]{3,2,1,0:T(1,128)S(1)}, u32[]{:S(2)}) copy-start(f32[8,16,1,256]{3,2,1,0:T(1,128)S(1)} %get-tuple-element.146) | copy-start | bytes 393220
  19.4 164.3 %copy-start.3 = (f32[8,16,1,256]{3,2,1,0:T(1,128)}, f32[8,16,1,256]{3,2,1,0:T(1,128)S(1)}, u32[]{:S(2)}) copy-start(f32[8,16,1,256]{3,2,1,0:T(1,128)S(1)} %get-tuple-element.147) | copy-start | bytes 393220
  212.3 46.9 %copy-start.38 = (s32[256]{0:T(256)S(1)}, s32[256]{0:T(256)}, u32[]{:S(2)}) copy-start(s32[256]{0:T(256)} %copy-done.37) | copy-start | bytes 3076
  308.7 429.6 %all-reduce.8.cloned.1.call-start = ((), (), s32[]{:S(2)}) async-start(), calls=%async_computation.1 | async-start | bytes 4194304 | tf_op jit(solution)/shard_map/psum | solution.py:144
  408.7 240.1 %copy-start.2 = (f32[8,16,8,512]{3,0,2,1:T(8,128)}, f32[8,16,8,512]{3,0,2,1:T(8,128)S(1)}, u32[]{:S(2)}) copy-start(f32[8,16,8,512]{3,0,2,1:T(8,128)S(1)} %multiply_add_fusion) | copy-start | bytes 6291460
  416.5 28.7 %copy-start.51 = (pred[256]{0:T(512)(128)(4,1)S(1)}, pred[256]{0:T(512)(128)(4,1)}, u32[]{:S(2)}) copy-start(pred[256]{0:T(512)(128)(4,1)} %copy-done.50) | copy-start | bytes 772
  438.1 16.0 %copy-start.48 = (pred[256]{0:T(512)(128)(4,1)S(1)}, pred[256]{0:T(512)(128)(4,1)}, u32[]{:S(2)}) copy-start(pred[256]{0:T(512)(128)(4,1)} %copy-done.47) | copy-start | bytes 772
  544.0 46.9 %copy-start.39 = (s32[256]{0:T(256)S(1)}, s32[256]{0:T(256)}, u32[]{:S(2)}) copy-start(s32[256]{0:T(256)} %copy-done.37) | copy-start | bytes 3076
  640.3 139.5 %all-reduce.10.cloned.1.call-start = ((), (), s32[]{:S(2)}) async-start(), calls=%async_computation.2 | async-start | bytes 2097152 | tf_op jit(solution)/shard_map/psum | solution.py:151
  648.9 144.8 %copy-start.35 = (f32[16,4]{0,1:T(4,128)}, f32[16,4]{0,1:T(4,128)S(1)}, u32[]{:S(2)}) copy-start(f32[16,4]{0,1:T(4,128)S(1)} %pad_maximum_fusion) | copy-start | bytes 772
  651.7 344.6 %all-reduce.14.cloned.1.call-start = ((), (), s32[]{:S(2)}) async-start(), calls=%async_computation.4 | async-start | bytes 2097152 | tf_op jit(solution)/shard_map/psum | solution.py:151
  793.6 27.8 %copy-start.52 = (pred[256]{0:T(512)(128)(4,1)S(1)}, pred[256]{0:T(512)(128)(4,1)}, u32[]{:S(2)}) copy-start(pred[256]{0:T(512)(128)(4,1)} %copy-done.50) | copy-start | bytes 772
  865.7 228.2 %all-reduce.12.cloned.1.call-start = ((), (), s32[]{:S(2)}) async-start(), calls=%async_computation.3 | async-start | bytes 4194304 | tf_op jit(solution)/shard_map/psum | solution.py:144
  898.5 46.9 %copy-start.40 = (s32[256]{0:T(256)S(1)}, s32[256]{0:T(256)}, u32[]{:S(2)}) copy-start(s32[256]{0:T(256)} %copy-done.37) | copy-start | bytes 3076
  (36 other events, 244.2 us)
Sparse Core Ops, SparseCore 0:
  10.7 77.0 all-gather.2
  308.8 97.0 all-reduce.5
  640.4 97.8 all-reduce.7
  740.4 39.3 all-reduce.9
  865.9 40.0 all-reduce.13
  995.4 98.4 all-reduce.11
